TPU v7x, 256 devices: a whole 4x4x8 slice. The times are simulated.
256 devices in a mesh: seq: 32 (over y, z_lo, core), head: 8 (over x, z_hi).
Axes of the slice: x: 4, y: 4, z: 8 (z_hi: 2, z_lo: 4; z = z_hi * 4 + z_lo), core: 2. Of those that a mesh axis runs over, the one named last changes fastest.
Arguments:
- tokens: bfloat16 [131072, 1024], P(('seq', 'head')), may hold values from -32 to 32
- w_qkv: bfloat16 [1024, 3072], P('seq'), may hold values from -0.1875 to 0.1875
- w_out: bfloat16 [1024, 1024], P('seq'), may hold values from -0.1875 to 0.1875
- neighbours: int32 [1024, 12], P('seq'), may hold values from 0 to 1023, as said below
Outputs:
- update: bfloat16 [131072, 1024], P(('seq', 'head'))
Inputs may be any that keep to these rules, and one draw needn't show every extreme that they name: Block b has grid coordinates z = b // 16, y = (b // 4) % 4, x = b % 4. Each row lists b itself first, then 11 different blocks among its 26 neighbours at offsets -1, 0, 1 in each coordinate (z taken modulo 1024 // 16, y and x modulo 4).
All inputs are finite; a program needn't handle non-finite values.
Results may differ from a plain program's by a relative error of at most 0.0065.
The roundings to bfloat16 on the way count: a program that leaves them out, or rounds other values in their place, can miss the bound.
Values may be sent and summed in bfloat16 or wider, within the bound.
A program may use at most 64 MiB of HBM per device.

v0:
```python
import math

import jax
import jax.numpy as jnp
from jax import lax
from jax.sharding import PartitionSpec as P

HEADS = 8
HD = 128
BLK = 128
NBR = 12
PB = 16


def padded_2(cells, sides, width):
    for axis, dim in sides:
        count = lax.axis_size(axis)
        head = lax.slice_in_dim(cells, 0, width, axis=dim)
        tail = lax.slice_in_dim(cells, cells.shape[dim] - width, cells.shape[dim], axis=dim)
        cells = jnp.concatenate(
            [
                lax.ppermute(tail, axis, [(i, (i + 1) % count) for i in range(count)]),
                cells,
                lax.ppermute(head, axis, [((i + 1) % count, i) for i in range(count)]),
            ],
            axis=dim,
        )
    return cells


def local(tokens, w_qkv, w_out, neighbours):
    head_count = lax.axis_size("head")
    seq_count = lax.axis_size("seq")
    per_device = HEADS // head_count
    local_rows = tokens.shape[0]
    slab_rows = local_rows * head_count
    full_qkv = lax.all_gather(w_qkv, "seq", axis=0, tiled=True)
    projected = jnp.dot(tokens, full_qkv, preferred_element_type=jnp.float32)
    projected = projected.astype(jnp.bfloat16).reshape(local_rows, 3, HEADS, HD)
    slab = lax.all_to_all(projected, "head", split_axis=2, concat_axis=0, tiled=True)
    queries = slab[:, 0]
    key_value = slab[:, 1:3]
    padded = padded_2(key_value, (("seq", 0),), PB * BLK)
    kv_blocks = padded.reshape(-1, BLK, 2, per_device, HD)
    block_count = neighbours.shape[0]
    first_block = lax.axis_index("seq") * block_count
    local_lists = jnp.mod(neighbours - first_block + PB, block_count * seq_count)
    group_blocks = 4
    scale = 1.0 / math.sqrt(HD)

    def attend(args):
        query_group, list_group = args
        picked = kv_blocks[list_group].reshape(group_blocks, NBR * BLK, 2, per_device, HD)
        keys = picked[:, :, 0]
        values = picked[:, :, 1]
        scores = (
            jnp.einsum("nqhd,nkhd->nhqk", query_group, keys, preferred_element_type=jnp.float32)
            * scale
        )
        largest = jnp.max(scores, axis=-1, keepdims=True)
        expo = jnp.exp(scores - largest)
        probs = (expo / jnp.sum(expo, axis=-1, keepdims=True)).astype(jnp.bfloat16)
        result = jnp.einsum("nhqk,nkhd->nqhd", probs, values, preferred_element_type=jnp.float32)
        return result.astype(jnp.bfloat16)

    grouped_q = queries.reshape(block_count // group_blocks, group_blocks, BLK, per_device, HD)
    grouped_l = local_lists.reshape(block_count // group_blocks, group_blocks, NBR)
    attended = lax.map(attend, (grouped_q, grouped_l)).reshape(slab_rows, per_device, HD)
    returned = lax.all_to_all(attended, "head", split_axis=0, concat_axis=1, tiled=True)
    flat = returned.reshape(local_rows, HEADS * HD)
    full_out = lax.all_gather(w_out, "seq", axis=0, tiled=True)
    update = jnp.dot(flat, full_out, preferred_element_type=jnp.float32)
    return update.astype(jnp.bfloat16)


def solution(mesh):
    return jax.shard_map(
        local,
        mesh=mesh,
        in_specs=(P(("seq", "head"), None), P("seq", None), P("seq", None), P("seq", None)),
        out_specs=P(("seq", "head"), None),
        check_vma=False,
    )
```

profile of v0, /device:TPU:69, one launch (start us, length us, event | category | flops | bytes accessed | tf_op | source)
XLA Modules:
  0.0 381.4 jit_solution(7192390426923187747)
XLA Ops:
  7.3 69.8 %all-gather.3.cloned.1.call-done = bf16[1024,3072]{1,0:T(8,128)(2,1)} async-done(((bf16[32,3072]{1,0:T(8,128)(2,1)}), bf16[1024,3072]{1,0:T(8,128)(2,1)}) %all-gather.3.cloned.1.call-update) | async-done | bytes 6291472 | tf_op jit(solution)/shard_map/all_gather | solution.py:37
  77.1 6.4 %fusion.29 = bf16[64,8,24,128]{3,1,2,0:T(8,128)(2,1)S(1)} fusion(bf16[512,1024]{1,0:T(8,128)(2,1)S(1)} %copy-done, bf16[1024,3072]{1,0:T(8,128)(2,1)} %all-gather.3.cloned.1.call-done), kind=kOutput, calls=%fused_computation.27 | convolution fusion | flops 3222798336 | bytes 10485760 | tf_op jit(solution)/shard_map/dot_general | solution.py:38
  85.1 81.1 %all_to_all.33 = bf16[512,3,8,128]{3,0,1,2:T(8,128)(2,1)S(1)} all-to-all(bf16[512,3,8,128]{3,0,1,2:T(8,128)(2,1)S(1)} %copy.20), channel_id=1, replica_groups=mesh['seq'=32,'head'=8] {'head'}, dimensions={2} | all-to-all | bytes 6291456 | tf_op jit(solution)/shard_map/all_to_all | solution.py:40
  175.1 14.4 %collective-permute-done = bf16[2048,2,1,128]{3,0,1,2:T(8,128)(2,1)} collective-permute-done((bf16[2048,2,1,128]{3,0,1,2:T(8,128)(2,1)}, bf16[2048,2,1,128]{3,0,1,2:T(8,128)(2,1)}, u32[]{:S(2)}, u32[]{:S(2)}) %collective-permute-start) | collective-permute-done | bytes 1048608 | tf_op jit(solution)/shard_map/ppermute | solution.py:22
  189.4 10.5 %collective-permute-done.1 = bf16[2048,2,1,128]{3,0,1,2:T(8,128)(2,1)} collective-permute-done((bf16[2048,2,1,128]{3,0,1,2:T(8,128)(2,1)S(1)}, bf16[2048,2,1,128]{3,0,1,2:T(8,128)(2,1)}, u32[]{:S(2)}, u32[]{:S(2)}) %collective-permute-start.1) | collective-permute-done | bytes 1048608 | tf_op jit(solution)/shard_map/ppermute | solution.py:24
  203.9 123.6 %while.10 = (s32[]{:T(128)}, bf16[8,4,128,1,128]{4,2,1,0,3:T(8,128)(2,1)S(1)}, s32[8,4,12]{2,1,0:T(4,128)S(1)}, bf16[64,128,2,1,128]{4,1,3,2,0:T(8,128)(2,1)}, bf16[8,4,128,1,128]{4,2,1,3,0:T(8,128)(2,1)}, /*index=5*/s32[]{:T(128)}) while((s32[]{:T(128)}, bf16[8,4,128,1,128]{4,2,1,0,3:T(8,128)(2,1)S(1)}, s32[8,4,12]{2,1,0:T(4,128)S(1)}, ...), condition=%wide.region_3.4_spmd, body=%wide.region_0.3_spmd.sunk | while | flops 609555072 | bytes 18229452 | solution.py:68
  204.0 4.9 %gather_fusion = bf16[48,128,2,128]{3,1,2,0:T(8,128)(2,1)} fusion(bf16[64,128,2,128]{3,1,2,0:T(8,128)(2,1)} %bitcast.87, s32[1024]{0:T(1024)S(1)} %pad_clamp_fusion.2), kind=kCustom, calls=%fused_computation.clone.1 | custom fusion | bytes 6291648 | tf_op jit(solution)/shard_map/while/body/eval_jaxpr/gather | solution.py:53
  208.9 4.0 %copy.35 = bf16[48,128,2,128]{3,1,0,2:T(8,128)(2,1)} copy(bf16[48,128,2,128]{3,1,2,0:T(8,128)(2,1)} %gather_fusion) | data formatting | bytes 6291456 | tf_op jit(solution)/shard_map/while/body/eval_jaxpr/gather | solution.py:53
  215.5 3.7 fusion.46
  219.5 4.9 %gather_fusion = bf16[48,128,2,128]{3,1,2,0:T(8,128)(2,1)} fusion(bf16[64,128,2,128]{3,1,2,0:T(8,128)(2,1)} %bitcast.87, s32[1024]{0:T(1024)S(1)} %pad_clamp_fusion.2), kind=kCustom, calls=%fused_computation.clone.1 | custom fusion | bytes 6291648 | tf_op jit(solution)/shard_map/while/body/eval_jaxpr/gather | solution.py:53
  224.4 4.0 %copy.35 = bf16[48,128,2,128]{3,1,0,2:T(8,128)(2,1)} copy(bf16[48,128,2,128]{3,1,2,0:T(8,128)(2,1)} %gather_fusion) | data formatting | bytes 6291456 | tf_op jit(solution)/shard_map/while/body/eval_jaxpr/gather | solution.py:53
  231.0 3.6 fusion.46
  234.9 4.9 %gather_fusion = bf16[48,128,2,128]{3,1,2,0:T(8,128)(2,1)} fusion(bf16[64,128,2,128]{3,1,2,0:T(8,128)(2,1)} %bitcast.87, s32[1024]{0:T(1024)S(1)} %pad_clamp_fusion.2), kind=kCustom, calls=%fused_computation.clone.1 | custom fusion | bytes 6291648 | tf_op jit(solution)/shard_map/while/body/eval_jaxpr/gather | solution.py:53
  239.9 4.0 %copy.35 = bf16[48,128,2,128]{3,1,0,2:T(8,128)(2,1)} copy(bf16[48,128,2,128]{3,1,2,0:T(8,128)(2,1)} %gather_fusion) | data formatting | bytes 6291456 | tf_op jit(solution)/shard_map/while/body/eval_jaxpr/gather | solution.py:53
  246.4 3.6 fusion.46
  250.4 4.9 %gather_fusion = bf16[48,128,2,128]{3,1,2,0:T(8,128)(2,1)} fusion(bf16[64,128,2,128]{3,1,2,0:T(8,128)(2,1)} %bitcast.87, s32[1024]{0:T(1024)S(1)} %pad_clamp_fusion.2), kind=kCustom, calls=%fused_computation.clone.1 | custom fusion | bytes 6291648 | tf_op jit(solution)/shard_map/while/body/eval_jaxpr/gather | solution.py:53
  255.3 4.0 %copy.35 = bf16[48,128,2,128]{3,1,0,2:T(8,128)(2,1)} copy(bf16[48,128,2,128]{3,1,2,0:T(8,128)(2,1)} %gather_fusion) | data formatting | bytes 6291456 | tf_op jit(solution)/shard_map/while/body/eval_jaxpr/gather | solution.py:53
  261.9 3.6 fusion.46
  265.8 4.9 %gather_fusion = bf16[48,128,2,128]{3,1,2,0:T(8,128)(2,1)} fusion(bf16[64,128,2,128]{3,1,2,0:T(8,128)(2,1)} %bitcast.87, s32[1024]{0:T(1024)S(1)} %pad_clamp_fusion.2), kind=kCustom, calls=%fused_computation.clone.1 | custom fusion | bytes 6291648 | tf_op jit(solution)/shard_map/while/body/eval_jaxpr/gather | solution.py:53
  270.7 4.0 %copy.35 = bf16[48,128,2,128]{3,1,0,2:T(8,128)(2,1)} copy(bf16[48,128,2,128]{3,1,2,0:T(8,128)(2,1)} %gather_fusion) | data formatting | bytes 6291456 | tf_op jit(solution)/shard_map/while/body/eval_jaxpr/gather | solution.py:53
  277.3 3.6 fusion.46
  281.3 4.9 %gather_fusion = bf16[48,128,2,128]{3,1,2,0:T(8,128)(2,1)} fusion(bf16[64,128,2,128]{3,1,2,0:T(8,128)(2,1)} %bitcast.87, s32[1024]{0:T(1024)S(1)} %pad_clamp_fusion.2), kind=kCustom, calls=%fused_computation.clone.1 | custom fusion | bytes 6291648 | tf_op jit(solution)/shard_map/while/body/eval_jaxpr/gather | solution.py:53
  286.2 4.0 %copy.35 = bf16[48,128,2,128]{3,1,0,2:T(8,128)(2,1)} copy(bf16[48,128,2,128]{3,1,2,0:T(8,128)(2,1)} %gather_fusion) | data formatting | bytes 6291456 | tf_op jit(solution)/shard_map/while/body/eval_jaxpr/gather | solution.py:53
  292.8 3.6 fusion.46
  296.7 4.9 %gather_fusion = bf16[48,128,2,128]{3,1,2,0:T(8,128)(2,1)} fusion(bf16[64,128,2,128]{3,1,2,0:T(8,128)(2,1)} %bitcast.87, s32[1024]{0:T(1024)S(1)} %pad_clamp_fusion.2), kind=kCustom, calls=%fused_computation.clone.1 | custom fusion | bytes 6291648 | tf_op jit(solution)/shard_map/while/body/eval_jaxpr/gather | solution.py:53
  301.6 4.0 %copy.35 = bf16[48,128,2,128]{3,1,0,2:T(8,128)(2,1)} copy(bf16[48,128,2,128]{3,1,2,0:T(8,128)(2,1)} %gather_fusion) | data formatting | bytes 6291456 | tf_op jit(solution)/shard_map/while/body/eval_jaxpr/gather | solution.py:53
  308.2 3.6 fusion.46
  312.1 4.9 %gather_fusion = bf16[48,128,2,128]{3,1,2,0:T(8,128)(2,1)} fusion(bf16[64,128,2,128]{3,1,2,0:T(8,128)(2,1)} %bitcast.87, s32[1024]{0:T(1024)S(1)} %pad_clamp_fusion.2), kind=kCustom, calls=%fused_computation.clone.1 | custom fusion | bytes 6291648 | tf_op jit(solution)/shard_map/while/body/eval_jaxpr/gather | solution.py:53
  317.1 4.0 %copy.35 = bf16[48,128,2,128]{3,1,0,2:T(8,128)(2,1)} copy(bf16[48,128,2,128]{3,1,2,0:T(8,128)(2,1)} %gather_fusion) | data formatting | bytes 6291456 | tf_op jit(solution)/shard_map/while/body/eval_jaxpr/gather | solution.py:53
  329.7 34.0 %all_to_all.34 = bf16[8,2,32768]{2,1,0:T(2,128)(2,1)} all-to-all(bf16[8,2,32768]{2,1,0:T(2,128)(2,1)S(1)} %reshape.97), channel_id=1, replica_groups=mesh['seq'=32,'head'=8] {'head'}, dimensions={0} | all-to-all | bytes 2097152 | tf_op jit(solution)/shard_map/all_to_all | solution.py:69
  363.8 4.3 %reshape.98 = bf16[4096,1,128]{2,1,0:T(2,128)(2,1)S(1)} reshape(bf16[8,2,32768]{2,1,0:T(2,128)(2,1)} %all_to_all.34) | data formatting | bytes 2097152
  370.7 3.8 %convolution_convert_fusion.1 = bf16[512,1024]{1,0:T(8,128)(2,1)} fusion(bf16[512,1024]{0,1:T(8,128)(2,1)S(1)} %bitcast.96, bf16[1024,1024]{1,0:T(8,128)(2,1)} %all-gather.5.cloned.1.call-done), kind=kOutput, calls=%fused_computation.28 | convolution fusion | flops 1074266112 | bytes 4194304 | tf_op jit(solution)/shard_map/dot_general | solution.py:72
  (78 shorter events, 46.1 us)
Async XLA Ops:
  6.5 70.6 %copy-start = (bf16[512,1024]{1,0:T(8,128)(2,1)S(1)}, bf16[512,1024]{1,0:T(8,128)(2,1)}, u32[]{:S(2)}) copy-start(bf16[512,1024]{1,0:T(8,128)(2,1)} %param.6) | copy-start | bytes 3145732
  6.5 70.5 %all-gather.3.cloned.1.call-start = ((), (), s32[]{:S(2)}) async-start(), calls=%async_computation.2 | async-start | bytes 6488064 | tf_op jit(solution)/shard_map/all_gather | solution.py:37
  7.3 363.4 %all-gather.5.cloned.1.call-start = ((), (), s32[]{:S(2)}) async-start(), calls=%async_computation.3 | async-start | bytes 2162688 | tf_op jit(solution)/shard_map/all_gather | solution.py:71
  166.4 1.7 copy-start.1
  166.4 4.5 %copy-start.2 = (s32[32,12]{0,1:T(8,128)S(1)}, s32[32,12]{0,1:T(8,128)}, u32[]{:S(2)}) copy-start(s32[32,12]{0,1:T(8,128)} %param.9) | copy-start | bytes 4612
  169.2 20.2 %collective-permute-start = (bf16[2048,2,1,128]{3,0,1,2:T(8,128)(2,1)}, bf16[2048,2,1,128]{3,0,1,2:T(8,128)(2,1)}, u32[]{:S(2)}, u32[]{:S(2)}) collective-permute-start(bf16[2048,2,1,128]{3,0,1,2:T(8,128)(2,1)} %get-tuple-element.53), channel_id=1, source_target_pairs={{0,8},{8,16},{16,24},{24,32},{32,40},{40,48},{48,56},{56,64},{64,7... | collective-permute-start | bytes 3145736 | tf_op jit(solution)/shard_map/ppermute | solution.py:22
  170.6 29.3 %collective-permute-start.1 = (bf16[2048,2,1,128]{3,0,1,2:T(8,128)(2,1)S(1)}, bf16[2048,2,1,128]{3,0,1,2:T(8,128)(2,1)}, u32[]{:S(2)}, u32[]{:S(2)}) collective-permute-start(bf16[2048,2,1,128]{3,0,1,2:T(8,128)(2,1)S(1)} %get-tuple-element.54), channel_id=1, source_target_pairs={{8,0},{16,8},{24,16},{32,24},{40,32},{48,40},{56,48},{64,56},{72,6... | collective-permute-start | bytes 3145736 | tf_op jit(solution)/shard_map/ppermute | solution.py:24
Sparse Core Ops, SparseCore 0:
  9.2 67.8 all-gather.2
  171.0 61.1 all-gather.4
where the time goes:
time: 386 us; the launch traced here: 381 us
  blocking collectives  115 us (30%)
  waiting for transfers between devices  95.4 us (25%)
  local copies, waits for them, and re-layouts  92.1 us (24%)
  matrix products  59.9 us (16%)
  between operations  13.5 us (3%)
    all_to_all x1, blocking collectives, local(): lax.all_to_all(projected, 'head', split_axis=2, concat_axis=0, tiled=True)  81.1 us
    gather x16, local copies, waits for them, and re-layouts, attend(): kv_blocks[list_group].reshape(group_blocks, NBR * BLK, 2, per_device, HD)  71.6 us
    all_gather x1, waiting for transfers between devices, local(): full_qkv = lax.all_gather(w_qkv, 'seq', axis=0, tiled=True)  69.8 us
    all_to_all x1, blocking collectives, local(): lax.all_to_all(attended, 'head', split_axis=0, concat_axis=1, tiled=True)  34 us
    dot_general x8, matrix products, attend(): jnp.einsum('nhqk,nkhd->nqhd', probs, values, preferred_element_type=jnp.f...  29.2 us
    sub x8, matrix products, attend(): expo = jnp.exp(scores - largest)  20.5 us
    ppermute x1, waiting for transfers between devices, padded_2(): lax.ppermute(tail, axis, [(i, (i + 1) % count) for i in range(count)])  14.4 us
    ppermute x1, waiting for transfers between devices, padded_2(): lax.ppermute(head, axis, [((i + 1) % count, i) for i in range(count)])  10.5 us
  transfers between devices with their start and end apart: 4, of which 3 were waited for; matrix products, arithmetic and copies ran while one was open for 37% of the time, Pallas kernels for 0%

commit v1 on v0

v1 whole, which is shorter than its diff:
```python
import functools
import math

import jax
import jax.numpy as jnp
from jax import lax
from jax.experimental import pallas as pl
from jax.experimental.pallas import tpu as pltpu
from jax.sharding import PartitionSpec as P

HEADS = 8
HD = 128
BLK = 128
NBR = 12
ROWS = 512
D = 1024
CHUNKS = 4
SLOTS = 9
SCALE = 1.0 / math.sqrt(HD)
MESH = pl.DeviceIdType.MESH


def gather_kernel(tok_ref, out_ref, local_sem, send_sem, recv_sem):
    seq = lax.axis_index("seq")
    head = lax.axis_index("head")
    seqs = 32
    x = head // 2
    zh = head % 2
    up = x // 2

    def at_x(bit):
        low = x % 2
        high = x // 2
        if bit & 1:
            low = 1 - low
        if bit & 2:
            high = 1 - high
        return {"seq": seq, "head": (high * 2 + low) * 2 + zh}

    step = 1 - 2 * up
    dev_z = {"seq": seq, "head": x * 2 + (1 - zh)}
    dev_1, dev_2, dev_3 = at_x(1), at_x(2), at_x(3)
    far_to = {"seq": lax.rem(seq + step + seqs, seqs), "head": head}
    far_from = {"seq": lax.rem(seq - step + seqs, seqs), "head": head}

    barrier = pltpu.get_barrier_semaphore()
    partners = (dev_z, dev_1, dev_2, dev_3, far_to, far_from)
    for dev in partners:
        pl.semaphore_signal(barrier, inc=1, device_id=dev, device_id_type=MESH)
    pl.semaphore_wait(barrier, len(partners))

    size = ROWS // CHUNKS

    def copy(kind, c, src, slot, dev):
        rows = pl.ds(c * size, size)
        return pltpu.make_async_remote_copy(
            src_ref=src.at[rows], dst_ref=out_ref.at[slot, rows],
            send_sem=send_sem.at[kind, c], recv_sem=recv_sem.at[kind, c],
            device_id=dev, device_id_type=MESH,
        )

    kinds = {
        0: (tok_ref, 1, dev_z),
        1: (tok_ref, 3, dev_2),
        2: (out_ref.at[1], 2, dev_1),
        3: (out_ref.at[1], 5, dev_3),
        4: (out_ref.at[2], 4, dev_3),
        5: (out_ref.at[5], 4, dev_1),
        6: (out_ref.at[3], 6, far_to),
        7: (out_ref.at[4], 7, far_to),
        8: (out_ref.at[5], 8, far_to),
    }
    made = {}

    def start(kind, c):
        src, slot, dev = kinds[kind]
        cp = copy(kind, c, src, slot, dev)
        cp.start()
        made[kind, c] = cp

    own = pltpu.make_async_copy(tok_ref, out_ref.at[0], local_sem)
    for c in range(CHUNKS):
        start(0, c)
    for c in range(CHUNKS):
        start(1, c)
    own.start()

    def middle(c):
        return 4 if c % 2 == 0 else 5

    for i in range(CHUNKS + 2):
        if i < CHUNKS:
            made[0, i].wait_recv()
            start(2, i)
            start(3, i)
            made[1, i].wait_recv()
            start(6, i)
        c = i - 1
        if 0 <= c < CHUNKS:
            made[2, c].wait_recv()
            made[3, c].wait_recv()
            start(middle(c), c)
            start(8, c)
        c = i - 2
        if 0 <= c < CHUNKS:
            made[middle(c), c].wait_recv()
            start(7, c)
    for c in range(CHUNKS):
        for kind in (6, 7, 8):
            made[kind, c].wait_recv()
    for cp in made.values():
        cp.wait_send()
    own.wait()


def gather_tokens(tokens):
    return pl.pallas_call(
        gather_kernel,
        out_shape=jax.ShapeDtypeStruct((SLOTS, ROWS, D), jnp.bfloat16),
        in_specs=[pl.BlockSpec(memory_space=pl.ANY)],
        out_specs=pl.BlockSpec(memory_space=pl.ANY),
        scratch_shapes=[
            pltpu.SemaphoreType.DMA,
            pltpu.SemaphoreType.DMA((9, CHUNKS)),
            pltpu.SemaphoreType.DMA((9, CHUNKS)),
        ],
        compiler_params=pltpu.CompilerParams(collective_id=0, has_side_effects=True),
        cost_estimate=pl.CostEstimate(flops=0, bytes_accessed=200 << 20, transcendentals=0),
        name="gather_tokens",
    )(tokens)


def attend_kernel(idx_ref, q_ref, k_ref, v_ref, w_ref, out_ref, att_ref):
    head = pl.program_id(0)
    for b in range(ROWS // BLK):
        q = q_ref[pl.ds(b * BLK, BLK), :]
        picks = [pl.multiple_of(idx_ref[b, j] * BLK, BLK) for j in range(NBR)]
        keys = jnp.concatenate([k_ref[pl.ds(i, BLK), :] for i in picks], axis=0)
        values = jnp.concatenate([v_ref[pl.ds(i, BLK), :] for i in picks], axis=0)
        scores = lax.dot_general(
            q, keys, (((1,), (1,)), ((), ())), preferred_element_type=jnp.float32
        ) * SCALE
        largest = jnp.max(scores, axis=-1, keepdims=True)
        expo = jnp.exp(scores - largest)
        total = jnp.sum(expo, axis=-1, keepdims=True)
        probs = (expo / total).astype(jnp.bfloat16)
        result = jnp.dot(probs, values, preferred_element_type=jnp.float32)
        att_ref[pl.ds(b * BLK, BLK), pl.ds(pl.multiple_of(head * HD, HD), HD)] = result.astype(jnp.bfloat16)

    @pl.when(head == HEADS - 1)
    def _():
        out_ref[...] = jnp.dot(
            att_ref[...], w_ref[...], preferred_element_type=jnp.float32
        ).astype(jnp.bfloat16)


def attend(idx, q, kv, w_out):
    total = SLOTS * ROWS
    return pl.pallas_call(
        attend_kernel,
        out_shape=jax.ShapeDtypeStruct((ROWS, D), jnp.bfloat16),
        grid_spec=pltpu.PrefetchScalarGridSpec(
            num_scalar_prefetch=1,
            grid=(HEADS,),
            in_specs=[
                pl.BlockSpec((ROWS, HD), lambda h, i: (0, h)),
                pl.BlockSpec((total, HD), lambda h, i: (0, h)),
                pl.BlockSpec((total, HD), lambda h, i: (0, HEADS + h)),
                pl.BlockSpec((D, D), lambda h, i: (0, 0)),
            ],
            out_specs=pl.BlockSpec((ROWS, D), lambda h, i: (0, 0)),
            scratch_shapes=[pltpu.VMEM((ROWS, D), jnp.bfloat16)],
        ),
        compiler_params=pltpu.CompilerParams(vmem_limit_bytes=40 << 20),
        name="attend",
    )(idx, q, kv, kv, w_out)


def local_lists(neighbours):
    seq = lax.axis_index("seq")
    head = lax.axis_index("head")
    rows = ROWS // BLK
    lists = lax.dynamic_slice_in_dim(neighbours, head * rows, rows, axis=0)
    up = head // 4
    plane = seq * 2 + up
    row = head % 4
    depth = 64
    step = jnp.mod(lists // 16 - plane, depth)
    near = jnp.where(up == 0, 1, depth - 1)
    kind = jnp.where(step == 0, 0, jnp.where(step == near, 1, 2))
    y = (lists // 4) % 4
    pair = row + 1 - 2 * (row % 2)
    which = jnp.where(y == row, 0, jnp.where(y == pair, 1, 2))
    return ((kind * 3 + which) * 4 + lists % 4).astype(jnp.int32)


def local(tokens, w_qkv, w_out, neighbours):
    full_qkv = lax.all_gather(w_qkv, "seq", axis=0, tiled=True)
    full_out = lax.all_gather(w_out, "seq", axis=0, tiled=True)
    idx = local_lists(neighbours)
    gathered = gather_tokens(tokens).reshape(SLOTS * ROWS, D)
    q = jnp.dot(tokens, full_qkv[:, :D], preferred_element_type=jnp.float32).astype(jnp.bfloat16)
    kv = jnp.dot(gathered, full_qkv[:, D:], preferred_element_type=jnp.float32).astype(jnp.bfloat16)
    return attend(idx, q, kv, full_out)


def solution(mesh):
    return jax.shard_map(
        local,
        mesh=mesh,
        in_specs=(P(("seq", "head"), None), P("seq", None), P("seq", None), P("seq", None)),
        out_specs=P(("seq", "head"), None),
        check_vma=False,
    )
```

time: 386 us -> 243 us (0.63)
  Pallas kernels: 0 us -> 127 us
  blocking collectives: 115 us -> 0 us
  local copies, waits for them, and re-layouts: 92.1 us -> 3.07 us
  matrix products: 59.9 us -> 27.4 us
  waiting for transfers between devices: 95.4 us -> 69.7 us
    pallas_call x0 -> x2, Pallas kernels: none -> 127 us  [the longest x1 102 us: gather_tokens(): pl.pallas_call(gather_kernel, out_shape=jax.ShapeDtypeStruct((SLOTS, ROWS...]
    all_to_all x2 -> x0, blocking collectives: 115 us -> none  [the longest x1 81.1 us: local(): lax.all_to_all(projected, 'head', split_axis=2, concat_axis=0, tiled=True)]
    gather x16 -> x0, local copies, waits for them, and re-layouts: 71.6 us -> none  [attend(): kv_blocks[list_group].reshape(group_blocks, NBR * BLK, 2, per_device, HD)]
    all_gather x1, waiting for transfers between devices: 69.8 us -> 37.2 us  [local(): full_qkv = lax.all_gather(w_qkv, 'seq', axis=0, tiled=True)]
    all_gather x1, waiting for transfers between devices: 0.02 us -> 31.1 us  [local(): full_out = lax.all_gather(w_out, 'seq', axis=0, tiled=True)]
    ppermute x2 -> x0, waiting for transfers between devices: 24.9 us -> none  [the longest x1 14.4 us: padded_2(): lax.ppermute(tail, axis, [(i, (i + 1) % count) for i in range(count)])]
    sub x8 -> x0, matrix products: 20.5 us -> none  [attend(): expo = jnp.exp(scores - largest)]
    dot_general x10 -> x2, matrix products: 39.4 us -> 27.4 us  [the longest x1 24.4 us: local(): jnp.dot(gathered, full_qkv[:, D:], preferred_element_type=jnp.float32)]
  transfers between devices with their start and end apart: 4 -> 2, of which waited for: 3 -> 2; matrix products, arithmetic and copies ran while one was open for 37% -> 12% of each run, Pallas kernels for 0% -> 42%
where the time goes in v1:
time: 243 us; the launch traced here: 240 us
  Pallas kernels  127 us (52%)
  waiting for transfers between devices  69.7 us (29%)
  matrix products  27.4 us (11%)
  between operations  13.5 us (6%)
  local copies, waits for them, and re-layouts  3.07 us (1%)
    pallas_call x1, Pallas kernels, gather_tokens(): pl.pallas_call(gather_kernel, out_shape=jax.ShapeDtypeStruct((SLOTS, ROWS...  102 us
    all_gather x1, waiting for transfers between devices, local(): full_qkv = lax.all_gather(w_qkv, 'seq', axis=0, tiled=True)  37.2 us
    all_gather x1, waiting for transfers between devices, local(): full_out = lax.all_gather(w_out, 'seq', axis=0, tiled=True)  31.1 us
    pallas_call x1, Pallas kernels, attend(): pl.pallas_call(attend_kernel, out_shape=jax.ShapeDtypeStruct((ROWS, D), j...  25 us
    dot_general x1, matrix products, local(): jnp.dot(gathered, full_qkv[:, D:], preferred_element_type=jnp.float32)  24.4 us
  transfers between devices with their start and end apart: 2, of which 2 were waited for; matrix products, arithmetic and copies ran while one was open for 12% of the time, Pallas kernels for 42%

profile of v1, /device:TPU:69, one launch (start us, length us, event | category | flops | bytes accessed | tf_op | source)
XLA Modules:
  0.0 240.3 jit_solution(11861682549944957480)
XLA Ops:
  6.5 0.0 copy-start
  6.5 0.0 copy-start.3
  6.5 0.0 all-gather.3.cloned.1.call-start
  6.5 0.7 all-gather.3.cloned.1.call-update
  7.3 0.0 all-gather.5.cloned.1.call-start
  7.3 0.7 all-gather.5.cloned.1.call-update
  8.1 0.0 copy-done
  8.1 0.1 constant_dynamic-slice_fusion
  8.1 0.1 copy.6
  8.2 101.6 %gather_tokens.1 = bf16[9,512,1024]{2,1,0:T(8,128)(2,1)} custom-call(bf16[512,1024]{1,0:T(8,128)(2,1)} %tok_ref.1), custom_call_target="tpu_custom_call" | custom-call | bytes 209715200 | tf_op jit(solution)/shard_map/gather_tokens/pallas_call | solution.py:117
  109.9 37.2 %all-gather.3.cloned.1.call-done = bf16[1024,3072]{1,0:T(8,128)(2,1)} async-done(((bf16[32,3072]{1,0:T(8,128)(2,1)}), bf16[1024,3072]{1,0:T(8,128)(2,1)}) %all-gather.3.cloned.1.call-update) | async-done | bytes 6291472 | tf_op jit(solution)/shard_map/all_gather | solution.py:198
  147.0 0.0 copy-done.3
  147.0 0.0 copy-start.2
  147.1 3.0 %fusion.3.q_ref = bf16[512,1024]{1,0:T(8,128)(2,1)S(1)} fusion(bf16[512,1024]{1,0:T(8,128)(2,1)S(1)} %copy-done.3, bf16[1024,3072]{1,0:T(8,128)(2,1)} %all-gather.3.cloned.1.call-done), kind=kOutput, calls=%fused_computation.4 | convolution fusion | flops 1074266112 | bytes 4194304 | tf_op jit(solution)/shard_map/dot_general | solution.py:202
  150.1 1.3 copy-done.2
  151.4 24.4 %convolution_convert_fusion.k_ref.v_ref = bf16[4608,2048]{1,0:T(8,128)(2,1)} fusion(bf16[4608,1024]{1,0:T(8,128)(2,1)S(1)} %bitcast.3, bf16[1024,3072]{1,0:T(8,128)(2,1)} %all-gather.3.cloned.1.call-done), kind=kOutput, calls=%fused_computation | convolution fusion | flops 19336790016 | bytes 32505856 | tf_op jit(solution)/shard_map/dot_general | solution.py:203
  175.8 31.1 %all-gather.5.cloned.1.call-done.w_ref = bf16[1024,1024]{1,0:T(8,128)(2,1)} async-done(((bf16[32,1024]{1,0:T(8,128)(2,1)}), bf16[1024,1024]{1,0:T(8,128)(2,1)}) %all-gather.5.cloned.1.call-update) | async-done | bytes 2097168 | tf_op jit(solution)/shard_map/all_gather | solution.py:199
  206.9 0.0 copy-start.1
  206.9 1.6 copy-done.1
  208.5 25.0 %attend.1 = bf16[512,1024]{1,0:T(8,128)(2,1)} custom-call(s32[4,12]{1,0:T(4,128)S(1)} %fusion.10.idx_ref, bf16[512,1024]{1,0:T(8,128)(2,1)S(1)} %fusion.3.q_ref, bf16[4608,2048]{1,0:T(8,128)(2,1)} %convolution_convert_fusion.k_ref.v_ref, bf16[4608,2048]{1,0:T(8,128)(2,1)} %convolution_convert_fusion.k_ref.v_ref, bf16[1024,1024]{1,0:T(8,128)(2,1)S(1)} %copy-done.1), custom_call_target="tpu_custom_call" | custom-call | tf_op jit(solution)/shard_map/attend/pallas_call | solution.py:159
  (1 shorter events, 0.0 us)
Async XLA Ops:
  6.5 1.5 copy-start
  6.5 140.5 %copy-start.3 = (bf16[512,1024]{1,0:T(8,128)(2,1)S(1)}, bf16[512,1024]{1,0:T(8,128)(2,1)}, u32[]{:S(2)}) copy-start(bf16[512,1024]{1,0:T(8,128)(2,1)} %tok_ref.1) | copy-start | bytes 3145732
  6.5 140.5 %all-gather.3.cloned.1.call-start = ((), (), s32[]{:S(2)}) async-start(), calls=%async_computation | async-start | bytes 6488064 | tf_op jit(solution)/shard_map/all_gather | solution.py:198
  7.3 199.6 %all-gather.5.cloned.1.call-start = ((), (), s32[]{:S(2)}) async-start(), calls=%async_computation.1 | async-start | bytes 2162688 | tf_op jit(solution)/shard_map/all_gather | solution.py:199
  147.0 4.3 %copy-start.2 = (bf16[9,512,1024]{2,1,0:T(8,128)(2,1)S(1)}, bf16[9,512,1024]{2,1,0:T(8,128)(2,1)}, u32[]{:S(2)}) copy-start(bf16[9,512,1024]{2,1,0:T(8,128)(2,1)} %gather_tokens.1) | copy-start | bytes 28311556
  206.9 1.6 copy-start.1
Sparse Core Ops, SparseCore 0:
  9.2 137.7 all-gather.2
  148.9 57.9 all-gather.4

commit v2 on v1

v2 whole, which is shorter than its diff:
```python
import math

import jax
import jax.numpy as jnp
from jax import lax
from jax.experimental import pallas as pl
from jax.experimental.pallas import tpu as pltpu
from jax.sharding import PartitionSpec as P

HEADS = 8
HD = 128
BLK = 128
NBR = 12
ROWS = 512
D = 1024
SLOTS = 9
FACTOR = math.log2(math.e) / math.sqrt(HD)
MESH = pl.DeviceIdType.MESH
CHUNKS = 8
SIZE = ROWS // CHUNKS
PIECES = 4
PIECE = ROWS // PIECES
TICKS = CHUNKS + 2
OWN, PAIR, THIRD = 0, 1, 2
NEAR, FAR = 3, 6


def layer_kernel(idx_ref, tok_ref, wqkv_ref, wout_ref, out_ref,
                 toks, wkv, wqo, kv, qs, att,
                 tsend, trecv, wsend, wrecv):
    seq = lax.axis_index("seq")
    head = lax.axis_index("head")
    y = seq // 8
    zl = (seq // 2) % 4
    core = seq % 2
    x = head // 2
    zh = head % 2
    z = zh * 4 + zl
    up = x // 2

    def device(dx=0, dy=0, dz=0, dc=0):
        nz = lax.rem(z + dz + 8, 8)
        ny = lax.rem(y + dy + 4, 4)
        nx = lax.rem(x + dx + 4, 4)
        nc = lax.rem(core + dc, 2)
        return {"seq": ny * 8 + lax.rem(nz, 4) * 2 + nc, "head": nx * 2 + nz // 4}

    def at_x(low, high):
        nl = lax.rem(x % 2 + low, 2)
        nh = lax.rem(up + high, 2)
        return {"seq": seq, "head": (nh * 2 + nl) * 2 + zh}

    step = 1 - 2 * up
    dev_z = device(dz=4)
    dev_1, dev_2, dev_3 = at_x(1, 0), at_x(0, 1), at_x(1, 1)
    far_to = {"seq": lax.rem(seq + step + 32, 32), "head": head}
    far_from = {"seq": lax.rem(seq - step + 32, 32), "head": head}
    w_z = (device(dz=1), device(dz=-1), device(dz=2))
    w_z_from = (device(dz=-1), device(dz=1), device(dz=-2))
    w_x = (device(dx=1), device(dx=-1), device(dx=2))
    w_y = (device(dy=1), device(dy=-1))
    sibling = device(dc=1)

    barrier = pltpu.get_barrier_semaphore()
    partners = (dev_z, dev_1, dev_2, dev_3, far_to, far_from) + w_z + w_z_from + w_x + w_y + (sibling,)
    for dev in partners:
        pl.semaphore_signal(barrier, inc=1, device_id=dev, device_id_type=MESH)

    wkv[y, zl, core] = wqkv_ref[:, D:]
    wqo[y, zl, core, :, :D] = wqkv_ref[:, :D]
    wqo[y, zl, core, :, D:] = wout_ref[...]
    toks[pl.ds(0, ROWS)] = tok_ref[...]
    pl.semaphore_wait(barrier, len(partners))

    weights = (wkv, wqo)
    quarter = pl.ds(pl.multiple_of(x * 512, 512), 512)
    made_w = {}

    def send_w(g, number, where, dev):
        cp = pltpu.make_async_remote_copy(
            src_ref=weights[g].at[where], dst_ref=weights[g].at[where],
            send_sem=wsend.at[g, number], recv_sem=wrecv.at[g, number],
            device_id=dev, device_id_type=MESH,
        )
        cp.start()
        made_w[g, number] = cp

    def got_w(g, *numbers):
        for number in numbers:
            made_w[g, number].wait_recv()

    every = slice(None)

    def w_stage_z(g):
        for j in range(3):
            send_w(g, j, (y, zl, core, every, quarter), w_z[j])

    def w_stage_x(g):
        for j, dz in enumerate((3, 1, 2)):
            got_w(g, j)
            for i in range(3):
                send_w(g, 3 + 3 * j + i, (y, lax.rem(zl + dz, 4), core, every, quarter), w_x[i])

    def w_stage_y(g):
        got_w(g, *range(3, 12))
        send_w(g, 12, (y, every, core), w_y[0])
        send_w(g, 13, (y, every, core), w_y[1])
        send_w(g, 16, (y, every, core), sibling)

    def w_stage_relay(g):
        down = lax.rem(y + 3, 4)
        above = lax.rem(y + 1, 4)
        got_w(g, 12)
        send_w(g, 14, (down, pl.ds(0, 2), core), w_y[0])
        send_w(g, 17, (down, every, core), sibling)
        got_w(g, 13)
        send_w(g, 15, (above, pl.ds(2, 2), core), w_y[1])
        send_w(g, 18, (above, every, core), sibling)

    def w_stage_last(g):
        across = lax.rem(y + 2, 4)
        got_w(g, 14)
        send_w(g, 19, (across, pl.ds(0, 2), core), sibling)
        got_w(g, 15)
        send_w(g, 20, (across, pl.ds(2, 2), core), sibling)

    def w_ready(g):
        got_w(g, *range(16, 21))

    kinds = {
        0: (OWN, PAIR, dev_z),
        1: (OWN, NEAR + OWN, dev_2),
        2: (PAIR, THIRD, dev_1),
        3: (PAIR, NEAR + THIRD, dev_3),
        4: (THIRD, NEAR + PAIR, dev_3),
        5: (NEAR + THIRD, NEAR + PAIR, dev_1),
        6: (NEAR + OWN, FAR + OWN, far_to),
        7: (NEAR + PAIR, FAR + PAIR, far_to),
        8: (NEAR + THIRD, FAR + THIRD, far_to),
    }
    made = {}

    def send(kind, c):
        src, dst, dev = kinds[kind]
        cp = pltpu.make_async_remote_copy(
            src_ref=toks.at[pl.ds(src * ROWS + c * SIZE, SIZE)],
            dst_ref=toks.at[pl.ds(dst * ROWS + c * SIZE, SIZE)],
            send_sem=tsend.at[kind, c], recv_sem=trecv.at[kind, c],
            device_id=dev, device_id_type=MESH,
        )
        cp.start()
        made[kind, c] = cp

    def middle(c):
        return 4 if c % 2 == 0 else 5

    def tick(i):
        if i < CHUNKS:
            made[0, i].wait_recv()
            send(2, i)
            send(3, i)
            made[1, i].wait_recv()
            send(6, i)
        c = i - 1
        if 0 <= c < CHUNKS:
            made[2, c].wait_recv()
            made[3, c].wait_recv()
            send(middle(c), c)
            send(8, c)
        c = i - 2
        if 0 <= c < CHUNKS:
            made[middle(c), c].wait_recv()
            send(7, c)

    per = CHUNKS // PIECES
    ready = {}
    for p in range(PIECES):
        last = per * (p + 1) - 1
        ready[OWN, p] = 0
        ready[PAIR, p] = last
        ready[NEAR + OWN, p] = last
        ready[THIRD, p] = last + 1
        ready[NEAR + THIRD, p] = last + 1
        ready[NEAR + PAIR, p] = last + 2
        ready[FAR + OWN, p] = last + 2
        ready[FAR + THIRD, p] = last + 3
        ready[FAR + PAIR, p] = last + 4
    pending = sorted(ready, key=lambda k: (ready[k], k))
    far_kind = {FAR + OWN: 6, FAR + PAIR: 7, FAR + THIRD: 8}

    def project(keys):
        offsets = []
        for slot, p in keys:
            if slot >= FAR:
                for c in range(per * p, per * (p + 1)):
                    made[far_kind[slot], c].wait_recv()
            offsets.append(slot * PIECES + p)

        def body(k, carry):
            n = k % 2
            which = k // 2
            row = jnp.int32(offsets[0])
            for j in range(1, len(offsets)):
                row = jnp.where(which == j, offsets[j], row)
            rows = pl.ds(pl.multiple_of(row * PIECE, PIECE), PIECE)
            cols = pl.ds(pl.multiple_of(n * D, D), D)
            w = wkv[:, :, :, :, cols].reshape(D, D)
            kv[row, :, cols] = jnp.dot(
                toks[rows, :], w, preferred_element_type=jnp.float32
            ).astype(jnp.bfloat16)
            return carry

        lax.fori_loop(0, 2 * len(offsets), body, 0)

    def project_up_to(t, limit):
        keys = [k for k in pending if ready[k] <= t][:limit]
        for k in keys:
            pending.remove(k)
        if keys:
            project(keys)

    w_stage_z(0)
    for c in range(CHUNKS):
        send(0, c)
    w_stage_z(1)
    w_stage_x(0)
    for c in range(CHUNKS):
        send(1, c)
    w_stage_y(0)
    tick(0)
    w_stage_x(1)
    tick(1)
    w_stage_relay(0)
    w_stage_y(1)
    tick(2)
    w_stage_last(0)
    tick(3)
    w_ready(0)
    project_up_to(3, 8)
    tick(4)
    project_up_to(4, 8)
    w_stage_relay(1)
    tick(5)
    project_up_to(5, 8)
    w_stage_last(1)
    tick(6)
    project_up_to(6, 8)
    w_ready(1)

    def q_body(n, carry):
        cols = pl.ds(pl.multiple_of(n * 512, 512), 512)
        w = wqo[:, :, :, :, cols].reshape(D, 512)
        qs[:, cols] = jnp.dot(
            toks[pl.ds(0, ROWS), :], w, preferred_element_type=jnp.float32
        ).astype(jnp.bfloat16)
        return carry

    lax.fori_loop(0, 2, q_body, 0)
    tick(7)
    project_up_to(7, 8)
    tick(8)
    project_up_to(8, 8)
    tick(9)
    project_up_to(9, 36)
    project_up_to(10, 36)
    project_up_to(11, 36)

    def one_head(h, carry):
        key_cols = pl.ds(pl.multiple_of(h * HD, HD), HD)
        value_cols = pl.ds(pl.multiple_of(h * HD + D, HD), HD)
        for b in range(ROWS // BLK):
            q = qs[pl.ds(b * BLK, BLK), key_cols]
            picks = [idx_ref[b, j] for j in range(NBR)]
            keys = jnp.concatenate([kv[i, :, key_cols] for i in picks], axis=0)
            values = jnp.concatenate([kv[i, :, value_cols] for i in picks], axis=0)
            scores = lax.dot_general(
                q, keys, (((1,), (1,)), ((), ())), preferred_element_type=jnp.float32
            )
            largest = jnp.max(scores, axis=-1, keepdims=True) * FACTOR
            expo = jnp.exp2(scores * FACTOR - largest)
            total = jnp.sum(expo, axis=-1, keepdims=True)
            result = jnp.dot(expo.astype(jnp.bfloat16), values, preferred_element_type=jnp.float32)
            att[pl.ds(b * BLK, BLK), key_cols] = (result * (1.0 / total)).astype(jnp.bfloat16)
        return carry

    lax.fori_loop(0, HEADS, one_head, 0)

    def out_body(n, carry):
        cols = pl.ds(pl.multiple_of(n * 512, 512), 512)
        w = wqo[:, :, :, :, pl.ds(pl.multiple_of(D + n * 512, 512), 512)].reshape(D, 512)
        out_ref[:, cols] = jnp.dot(
            att[...], w, preferred_element_type=jnp.float32
        ).astype(jnp.bfloat16)
        return carry

    lax.fori_loop(0, 2, out_body, 0)
    for cp in made.values():
        cp.wait_send()
    for cp in made_w.values():
        cp.wait_send()


def layer(idx, tokens, w_qkv, w_out):
    vmem = pl.BlockSpec(memory_space=pltpu.VMEM)
    bf16 = jnp.bfloat16
    return pl.pallas_call(
        layer_kernel,
        out_shape=jax.ShapeDtypeStruct((ROWS, D), bf16),
        in_specs=[pl.BlockSpec(memory_space=pltpu.SMEM), vmem, vmem, vmem],
        out_specs=vmem,
        scratch_shapes=[
            pltpu.VMEM((SLOTS * ROWS, D), bf16),
            pltpu.VMEM((4, 4, 2, 32, 2 * D), bf16),
            pltpu.VMEM((4, 4, 2, 32, 2 * D), bf16),
            pltpu.VMEM((SLOTS * ROWS // BLK, BLK, 2 * D), bf16),
            pltpu.VMEM((ROWS, D), bf16),
            pltpu.VMEM((ROWS, D), bf16),
            pltpu.SemaphoreType.DMA((9, CHUNKS)),
            pltpu.SemaphoreType.DMA((9, CHUNKS)),
            pltpu.SemaphoreType.DMA((2, 21)),
            pltpu.SemaphoreType.DMA((2, 21)),
        ],
        compiler_params=pltpu.CompilerParams(
            collective_id=0, has_side_effects=True, vmem_limit_bytes=56 << 20
        ),
        name="layer",
    )(idx, tokens, w_qkv, w_out)


def local_lists(neighbours):
    seq = lax.axis_index("seq")
    head = lax.axis_index("head")
    rows = ROWS // BLK
    lists = lax.dynamic_slice_in_dim(neighbours, head * rows, rows, axis=0)
    up = head // 4
    plane = seq * 2 + up
    row = head % 4
    depth = 64
    step = jnp.mod(lists // 16 - plane, depth)
    near = jnp.where(up == 0, 1, depth - 1)
    kind = jnp.where(step == 0, 0, jnp.where(step == near, 1, 2))
    y = (lists // 4) % 4
    pair = row + 1 - 2 * (row % 2)
    which = jnp.where(y == row, 0, jnp.where(y == pair, 1, 2))
    return ((kind * 3 + which) * 4 + lists % 4).astype(jnp.int32)


def local(tokens, w_qkv, w_out, neighbours):
    return layer(local_lists(neighbours), tokens, w_qkv, w_out)


def solution(mesh):
    return jax.shard_map(
        local,
        mesh=mesh,
        in_specs=(P(("seq", "head"), None), P("seq", None), P("seq", None), P("seq", None)),
        out_specs=P(("seq", "head"), None),
        check_vma=False,
    )
```

time: 243 us -> 171 us (0.70)
  the two profiles are of different devices: /device:TPU:69 before, /device:TPU:24 now
where the time goes in v2:
time: 171 us; the launch traced here: 170 us
  Pallas kernels  167 us (98%)
  local copies, waits for them, and re-layouts  3.13 us (2%)
    pallas_call x1, Pallas kernels, layer(): pl.pallas_call(layer_kernel, out_shape=jax.ShapeDtypeStruct((ROWS, D), bf...  167 us

profile of v2, /device:TPU:24, one launch (start us, length us, event | category | flops | bytes accessed | tf_op | source)
XLA Modules:
  0.0 170.4 jit_solution(15590306477463800309)
XLA Ops:
  0.0 0.0 copy-start
  0.0 0.7 copy-done
  0.7 0.1 constant_dynamic-slice_fusion
  0.8 0.1 copy.6
  0.9 0.6 fusion.4.idx_ref
  1.5 166.7 %layer.1 = bf16[512,1024]{1,0:T(8,128)(2,1)} custom-call(s32[4,12]{1,0:T(4,128)} %fusion.4.idx_ref, bf16[512,1024]{1,0:T(8,128)(2,1)} %tok_ref.1, bf16[32,3072]{1,0:T(8,128)(2,1)} %wqkv_ref.1, bf16[32,1024]{1,0:T(8,128)(2,1)} %wout_ref.1), custom_call_target="tpu_custom_call" | custom-call | tf_op jit(solution)/shard_map/layer/pallas_call | solution.py:306
  168.2 2.3 %copy.8 = bf16[512,1024]{1,0:T(8,128)(2,1)} copy(bf16[512,1024]{1,0:T(8,128)(2,1)} %layer.1) | data formatting | bytes 2097152
Async XLA Ops:
  0.0 0.7 copy-start

commit v3 on v2

--- a/solution.py
+++ b/solution.py
@@ -20,14 +20,16 @@
 SIZE = ROWS // CHUNKS
 PIECES = 4
 PIECE = ROWS // PIECES
-TICKS = CHUNKS + 2
+AHEAD = 3
+NEAR_AHEAD = 2
+RELAYED = (1, 4, 6)
 OWN, PAIR, THIRD = 0, 1, 2
 NEAR, FAR = 3, 6
 
 
 def layer_kernel(idx_ref, tok_ref, wqkv_ref, wout_ref, out_ref,
                  toks, wkv, wqo, kv, qs, att,
-                 tsend, trecv, wsend, wrecv):
+                 relayed, tsend, trecv, wsend, wrecv):
     seq = lax.axis_index("seq")
     head = lax.axis_index("head")
     y = seq // 8
@@ -53,8 +55,21 @@
     step = 1 - 2 * up
     dev_z = device(dz=4)
     dev_1, dev_2, dev_3 = at_x(1, 0), at_x(0, 1), at_x(1, 1)
-    far_to = {"seq": lax.rem(seq + step + 32, 32), "head": head}
-    far_from = {"seq": lax.rem(seq - step + 32, 32), "head": head}
+    end = lax.rem(seq, 8)
+    cross_to = jnp.where(end == 7 * (1 - up), 1, 0)
+    cross_from = jnp.where(end == 7 * up, 1, 0)
+    seq_to = lax.rem(seq + step + 32, 32)
+    seq_from = lax.rem(seq - step + 32, 32)
+
+    def across(seq_at, low, turn):
+        return {"seq": seq_at, "head": (up * 2 + lax.rem(x % 2 + low, 2)) * 2 + lax.rem(zh + turn, 2)}
+
+    far_to = across(seq_to, 0, cross_to)
+    far_to_third = across(seq_to, cross_to, cross_to)
+    far_from = across(seq_from, 0, cross_from)
+    far_from_third = across(seq_from, cross_from, cross_from)
+    relay_to, relay_from = device(dz=-step), device(dz=step)
+    onward_to, onward_from = device(dz=-3 * step), device(dz=3 * step)
     w_z = (device(dz=1), device(dz=-1), device(dz=2))
     w_z_from = (device(dz=-1), device(dz=1), device(dz=-2))
     w_x = (device(dx=1), device(dx=-1), device(dx=2))
@@ -62,7 +77,8 @@
     sibling = device(dc=1)
 
     barrier = pltpu.get_barrier_semaphore()
-    partners = (dev_z, dev_1, dev_2, dev_3, far_to, far_from) + w_z + w_z_from + w_x + w_y + (sibling,)
+    partners = (dev_z, dev_1, dev_2, dev_3, far_to, far_from, far_to_third, far_from_third)
+    partners += (onward_to, onward_from) + w_z + w_z_from + w_x + w_y + (sibling,)
     for dev in partners:
         pl.semaphore_signal(barrier, inc=1, device_id=dev, device_id_type=MESH)
 
@@ -128,48 +144,78 @@
         got_w(g, *range(16, 21))
 
     kinds = {
-        0: (OWN, PAIR, dev_z),
-        1: (OWN, NEAR + OWN, dev_2),
-        2: (PAIR, THIRD, dev_1),
-        3: (PAIR, NEAR + THIRD, dev_3),
-        4: (THIRD, NEAR + PAIR, dev_3),
-        5: (NEAR + THIRD, NEAR + PAIR, dev_1),
-        6: (NEAR + OWN, FAR + OWN, far_to),
-        7: (NEAR + PAIR, FAR + PAIR, far_to),
-        8: (NEAR + THIRD, FAR + THIRD, far_to),
+        0: (OWN, PAIR, 0, dev_z),
+        1: (OWN, NEAR + OWN, 1, dev_2),
+        2: (PAIR, THIRD, 2, dev_1),
+        3: (PAIR, NEAR + THIRD, 3, dev_3),
+        4: (THIRD, NEAR + PAIR, 4, dev_3),
+        5: (NEAR + THIRD, NEAR + PAIR, 4, dev_1),
+        6: (NEAR + OWN, FAR + OWN + cross_to, 6 + cross_to, far_to),
+        7: (NEAR + PAIR, FAR + PAIR - cross_to, 7 - cross_to, far_to),
+        8: (NEAR + THIRD - 2 * cross_to, FAR + THIRD, 8, far_to_third),
     }
-    made = {}
-
-    def send(kind, c):
-        src, dst, dev = kinds[kind]
+    made = []
+
+    def rows_of(slot, c):
+        return pl.ds(pl.multiple_of(slot * ROWS + c * SIZE, SIZE), SIZE)
+
+    def move(src, dst, kind, wait_row, c, dev):
         cp = pltpu.make_async_remote_copy(
-            src_ref=toks.at[pl.ds(src * ROWS + c * SIZE, SIZE)],
-            dst_ref=toks.at[pl.ds(dst * ROWS + c * SIZE, SIZE)],
-            send_sem=tsend.at[kind, c], recv_sem=trecv.at[kind, c],
+            src_ref=src, dst_ref=dst, send_sem=tsend.at[kind, c], recv_sem=trecv.at[wait_row, c],
             device_id=dev, device_id_type=MESH,
         )
         cp.start()
-        made[kind, c] = cp
-
-    def middle(c):
-        return 4 if c % 2 == 0 else 5
+        made.append(cp)
+
+    def send(kind, c):
+        src, dst, wait_row, dev = kinds[kind]
+        move(toks.at[rows_of(src, c)], toks.at[rows_of(dst, c)], kind, wait_row, c, dev)
+
+    slot_of_row = (PAIR, NEAR + OWN, THIRD, NEAR + THIRD, NEAR + PAIR, None, FAR + OWN, FAR + PAIR, FAR + THIRD)
+
+    def wait_in(ref, row, c):
+        pltpu.make_async_remote_copy(
+            src_ref=ref, dst_ref=ref, send_sem=tsend.at[row, c], recv_sem=trecv.at[row, c],
+            device_id=dev_z, device_id_type=MESH,
+        ).wait_recv()
+
+    def arrived(row, c):
+        wait_in(toks.at[rows_of(slot_of_row[row], c)], row, c)
+
+    def send_pair(c):
+        if c >= CHUNKS:
+            return
+        if c in RELAYED:
+            move(toks.at[rows_of(OWN, c)], relayed.at[RELAYED.index(c)], 0, 9, c, relay_to)
+        else:
+            send(0, c)
+
+    def pass_on(c):
+        if c in RELAYED:
+            buffer = relayed.at[RELAYED.index(c)]
+            wait_in(buffer, 9, c)
+            move(buffer, toks.at[rows_of(PAIR, c)], 9, 0, c, onward_to)
 
     def tick(i):
         if i < CHUNKS:
-            made[0, i].wait_recv()
+            pass_on(i + 2)
+            arrived(0, i)
+            send_pair(i + AHEAD)
             send(2, i)
             send(3, i)
-            made[1, i].wait_recv()
+            arrived(1, i)
+            if i + NEAR_AHEAD < CHUNKS:
+                send(1, i + NEAR_AHEAD)
             send(6, i)
         c = i - 1
         if 0 <= c < CHUNKS:
-            made[2, c].wait_recv()
-            made[3, c].wait_recv()
-            send(middle(c), c)
+            arrived(2, c)
+            arrived(3, c)
+            send(4 if c % 2 == 0 else 5, c)
             send(8, c)
         c = i - 2
         if 0 <= c < CHUNKS:
-            made[middle(c), c].wait_recv()
+            arrived(4, c)
             send(7, c)
 
     per = CHUNKS // PIECES
@@ -182,18 +228,17 @@
         ready[THIRD, p] = last + 1
         ready[NEAR + THIRD, p] = last + 1
         ready[NEAR + PAIR, p] = last + 2
-        ready[FAR + OWN, p] = last + 2
+        ready[FAR + OWN, p] = last + 4
         ready[FAR + THIRD, p] = last + 3
         ready[FAR + PAIR, p] = last + 4
     pending = sorted(ready, key=lambda k: (ready[k], k))
-    far_kind = {FAR + OWN: 6, FAR + PAIR: 7, FAR + THIRD: 8}
 
     def project(keys):
         offsets = []
         for slot, p in keys:
             if slot >= FAR:
                 for c in range(per * p, per * (p + 1)):
-                    made[far_kind[slot], c].wait_recv()
+                    arrived(slot, c)
             offsets.append(slot * PIECES + p)
 
         def body(k, carry):
@@ -220,12 +265,14 @@
             project(keys)
 
     w_stage_z(0)
-    for c in range(CHUNKS):
-        send(0, c)
+    for c in range(AHEAD):
+        send_pair(c)
     w_stage_z(1)
     w_stage_x(0)
-    for c in range(CHUNKS):
+    for c in range(NEAR_AHEAD):
         send(1, c)
+    pass_on(0)
+    pass_on(1)
     w_stage_y(0)
     tick(0)
     w_stage_x(1)
@@ -294,7 +341,7 @@
         return carry
 
     lax.fori_loop(0, 2, out_body, 0)
-    for cp in made.values():
+    for cp in made:
         cp.wait_send()
     for cp in made_w.values():
         cp.wait_send()
@@ -315,8 +362,9 @@
             pltpu.VMEM((SLOTS * ROWS // BLK, BLK, 2 * D), bf16),
             pltpu.VMEM((ROWS, D), bf16),
             pltpu.VMEM((ROWS, D), bf16),
-            pltpu.SemaphoreType.DMA((9, CHUNKS)),
-            pltpu.SemaphoreType.DMA((9, CHUNKS)),
+            pltpu.VMEM((len(RELAYED), SIZE, D), bf16),
+            pltpu.SemaphoreType.DMA((10, CHUNKS)),
+            pltpu.SemaphoreType.DMA((10, CHUNKS)),
             pltpu.SemaphoreType.DMA((2, 21)),
             pltpu.SemaphoreType.DMA((2, 21)),
         ],

time: 171 us -> 139 us (0.81)
  the two profiles are of different devices: /device:TPU:24 before, /device:TPU:69 now
where the time goes in v3:
time: 139 us
  Pallas kernels  135 us (97%)
  local copies, waits for them, and re-layouts  3.13 us (2%)
    pallas_call x1, Pallas kernels, layer(): pl.pallas_call(layer_kernel, out_shape=jax.ShapeDtypeStruct((ROWS, D), bf...  135 us
    unnamed x4, local copies, waits for them, and re-layouts  3.05 us

profile of v3, /device:TPU:69, one launch (start us, length us, event | category | flops | bytes accessed | tf_op | source)
XLA Modules:
  0.0 138.6 jit_solution(5785584047450472702)
XLA Ops:
  0.0 0.0 copy-start
  0.0 0.7 copy-done
  0.7 0.1 constant_dynamic-slice_fusion
  0.8 0.1 copy.6
  0.9 0.6 fusion.4.idx_ref
  1.5 134.9 %layer.1 = bf16[512,1024]{1,0:T(8,128)(2,1)} custom-call(s32[4,12]{1,0:T(4,128)} %fusion.4.idx_ref, bf16[512,1024]{1,0:T(8,128)(2,1)} %tok_ref.1, bf16[32,3072]{1,0:T(8,128)(2,1)} %wqkv_ref.1, bf16[32,1024]{1,0:T(8,128)(2,1)} %wout_ref.1), custom_call_target="tpu_custom_call" | custom-call | tf_op jit(solution)/shard_map/layer/pallas_call | solution.py:353
  136.4 2.3 %copy.8 = bf16[512,1024]{1,0:T(8,128)(2,1)} copy(bf16[512,1024]{1,0:T(8,128)(2,1)} %layer.1) | data formatting | bytes 2097152
Async XLA Ops:
  0.0 0.7 copy-start

commit v4 on v3

--- a/solution.py
+++ b/solution.py
@@ -21,7 +21,7 @@
 PIECES = 4
 PIECE = ROWS // PIECES
 AHEAD = 3
-NEAR_AHEAD = 2
+NEAR_AHEAD = 3
 RELAYED = (1, 4, 6)
 OWN, PAIR, THIRD = 0, 1, 2
 NEAR, FAR = 3, 6
@@ -312,22 +312,34 @@
     project_up_to(10, 36)
     project_up_to(11, 36)
 
+    ones = jnp.ones((NBR * BLK, HD), jnp.bfloat16)
+
     def one_head(h, carry):
         key_cols = pl.ds(pl.multiple_of(h * HD, HD), HD)
         value_cols = pl.ds(pl.multiple_of(h * HD + D, HD), HD)
-        for b in range(ROWS // BLK):
+
+        def score(b):
             q = qs[pl.ds(b * BLK, BLK), key_cols]
-            picks = [idx_ref[b, j] for j in range(NBR)]
-            keys = jnp.concatenate([kv[i, :, key_cols] for i in picks], axis=0)
-            values = jnp.concatenate([kv[i, :, value_cols] for i in picks], axis=0)
-            scores = lax.dot_general(
+            keys = jnp.concatenate([kv[idx_ref[b, j], :, key_cols] for j in range(NBR)], axis=0)
+            return lax.dot_general(
                 q, keys, (((1,), (1,)), ((), ())), preferred_element_type=jnp.float32
             )
+
+        def finish(b, scores):
+            values = jnp.concatenate([kv[idx_ref[b, j], :, value_cols] for j in range(NBR)], axis=0)
             largest = jnp.max(scores, axis=-1, keepdims=True) * FACTOR
-            expo = jnp.exp2(scores * FACTOR - largest)
-            total = jnp.sum(expo, axis=-1, keepdims=True)
-            result = jnp.dot(expo.astype(jnp.bfloat16), values, preferred_element_type=jnp.float32)
-            att[pl.ds(b * BLK, BLK), key_cols] = (result * (1.0 / total)).astype(jnp.bfloat16)
+            expo = jnp.exp2(scores * FACTOR - largest).astype(jnp.bfloat16)
+            both = jnp.dot(
+                expo, jnp.concatenate([values, ones], axis=1), preferred_element_type=jnp.float32
+            )
+            att[pl.ds(b * BLK, BLK), key_cols] = (both[:, :HD] / both[:, HD:]).astype(jnp.bfloat16)
+
+        scores = score(0)
+        for b in range(1, ROWS // BLK):
+            following = score(b)
+            finish(b - 1, scores)
+            scores = following
+        finish(ROWS // BLK - 1, scores)
         return carry
 
     lax.fori_loop(0, HEADS, one_head, 0)

time: 139 us -> 134 us (0.964); the launches traced: 139 us -> 131 us
  Pallas kernels: 135 us -> 127 us
    pallas_call x1, Pallas kernels: 135 us -> 127 us  [layer(): pl.pallas_call(layer_kernel, out_shape=jax.ShapeDtypeStruct((ROWS, D), bf...]
where the time goes in v4:
time: 134 us; the launch traced here: 131 us
  Pallas kernels  127 us (95%)
  local copies, waits for them, and re-layouts  3.13 us (2%)
    pallas_call x1, Pallas kernels, layer(): pl.pallas_call(layer_kernel, out_shape=jax.ShapeDtypeStruct((ROWS, D), bf...  127 us
    unnamed x4, local copies, waits for them, and re-layouts  3.05 us

profile of v4, /device:TPU:69, one launch (start us, length us, event | category | flops | bytes accessed | tf_op | source)
XLA Modules:
  0.0 131.0 jit_solution(8586988453240098700)
XLA Ops:
  0.0 0.0 copy-start
  0.0 0.7 copy-done
  0.7 0.1 constant_dynamic-slice_fusion
  0.8 0.1 copy.6
  0.9 0.6 fusion.4.idx_ref
  1.5 127.2 %layer.1 = bf16[512,1024]{1,0:T(8,128)(2,1)} custom-call(s32[4,12]{1,0:T(4,128)} %fusion.4.idx_ref, bf16[512,1024]{1,0:T(8,128)(2,1)} %tok_ref.1, bf16[32,3072]{1,0:T(8,128)(2,1)} %wqkv_ref.1, bf16[32,1024]{1,0:T(8,128)(2,1)} %wout_ref.1), custom_call_target="tpu_custom_call" | custom-call | tf_op jit(solution)/shard_map/layer/pallas_call | solution.py:365
  128.7 2.3 %copy.8 = bf16[512,1024]{1,0:T(8,128)(2,1)} copy(bf16[512,1024]{1,0:T(8,128)(2,1)} %layer.1) | data formatting | bytes 2097152
Async XLA Ops:
  0.0 0.7 copy-start

commit v5 on v4

--- a/solution.py
+++ b/solution.py
@@ -265,9 +265,9 @@
             project(keys)
 
     w_stage_z(0)
+    w_stage_z(1)
     for c in range(AHEAD):
         send_pair(c)
-    w_stage_z(1)
     w_stage_x(0)
     for c in range(NEAR_AHEAD):
         send(1, c)
@@ -308,9 +308,8 @@
     tick(8)
     project_up_to(8, 8)
     tick(9)
-    project_up_to(9, 36)
-    project_up_to(10, 36)
-    project_up_to(11, 36)
+    while pending:
+        project_up_to(99, 3)
 
     ones = jnp.ones((NBR * BLK, HD), jnp.bfloat16)
 

time: 134 us -> 135 us (level)
  the two profiles are of different devices: /device:TPU:69 before, /device:TPU:87 now
where the time goes in v5:
time: 135 us
  Pallas kernels  132 us (98%)
  local copies, waits for them, and re-layouts  3.13 us (2%)
    pallas_call x1, Pallas kernels, layer(): pl.pallas_call(layer_kernel, out_shape=jax.ShapeDtypeStruct((ROWS, D), bf...  132 us
    unnamed x4, local copies, waits for them, and re-layouts  3.05 us

profile of v5, /device:TPU:87, one launch (start us, length us, event | category | flops | bytes accessed | tf_op | source)
XLA Modules:
  0.0 135.3 jit_solution(16171659029937681008)
XLA Ops:
  0.0 0.0 copy-start
  0.0 0.7 copy-done
  0.7 0.1 constant_dynamic-slice_fusion
  0.8 0.1 copy.6
  0.9 0.6 fusion.4.idx_ref
  1.5 131.5 %layer.1 = bf16[512,1024]{1,0:T(8,128)(2,1)} custom-call(s32[4,12]{1,0:T(4,128)} %fusion.4.idx_ref, bf16[512,1024]{1,0:T(8,128)(2,1)} %tok_ref.1, bf16[32,3072]{1,0:T(8,128)(2,1)} %wqkv_ref.1, bf16[32,1024]{1,0:T(8,128)(2,1)} %wout_ref.1), custom_call_target="tpu_custom_call" | custom-call | tf_op jit(solution)/shard_map/layer/pallas_call | solution.py:364
  133.0 2.3 %copy.8 = bf16[512,1024]{1,0:T(8,128)(2,1)} copy(bf16[512,1024]{1,0:T(8,128)(2,1)} %layer.1) | data formatting | bytes 2097152
Async XLA Ops:
  0.0 0.7 copy-start

commit v6 on v5

--- a/solution.py
+++ b/solution.py
@@ -265,9 +265,9 @@
             project(keys)
 
     w_stage_z(0)
-    w_stage_z(1)
     for c in range(AHEAD):
         send_pair(c)
+    w_stage_z(1)
     w_stage_x(0)
     for c in range(NEAR_AHEAD):
         send(1, c)

time: 135 us -> 134 us (level)
  the two profiles are of different devices: /device:TPU:87 before, /device:TPU:69 now
where the time goes in v6:
time: 134 us; the launch traced here: 132 us
  Pallas kernels  128 us (96%)
  local copies, waits for them, and re-layouts  3.13 us (2%)
    pallas_call x1, Pallas kernels, layer(): pl.pallas_call(layer_kernel, out_shape=jax.ShapeDtypeStruct((ROWS, D), bf...  128 us
    unnamed x4, local copies, waits for them, and re-layouts  3.05 us

profile of v6, /device:TPU:69, one launch (start us, length us, event | category | flops | bytes accessed | tf_op | source)
XLA Modules:
  0.0 131.9 jit_solution(11447868624281479378)
XLA Ops:
  0.0 0.0 copy-start
  0.0 0.7 copy-done
  0.7 0.1 constant_dynamic-slice_fusion
  0.8 0.1 copy.6
  0.9 0.6 fusion.4.idx_ref
  1.5 128.2 %layer.1 = bf16[512,1024]{1,0:T(8,128)(2,1)} custom-call(s32[4,12]{1,0:T(4,128)} %fusion.4.idx_ref, bf16[512,1024]{1,0:T(8,128)(2,1)} %tok_ref.1, bf16[32,3072]{1,0:T(8,128)(2,1)} %wqkv_ref.1, bf16[32,1024]{1,0:T(8,128)(2,1)} %wout_ref.1), custom_call_target="tpu_custom_call" | custom-call | tf_op jit(solution)/shard_map/layer/pallas_call | solution.py:364
  129.6 2.3 %copy.8 = bf16[512,1024]{1,0:T(8,128)(2,1)} copy(bf16[512,1024]{1,0:T(8,128)(2,1)} %layer.1) | data formatting | bytes 2097152
Async XLA Ops:
  0.0 0.7 copy-start
